TPU v7x, 256 devices: a whole 4x4x8 slice. The times are simulated.
256 devices in a mesh: group: 4 (over x), member: 64 (over y, z, core).
Axes of the slice: x: 4, y: 4, z: 8, core: 2. Of those that a mesh axis runs over, the one named last changes fastest.
Arguments:
- load: float32 [3, 7, 7, 8, 32768], P(None, None, None, None, ('group', 'member')), may hold values from -6 to 6
- stiffness_dir: float32 [3, 32768], P(None, ('group', 'member')), may hold values from 0.5 to 4
- bulk_ratio: float32 [32768], P(('group', 'member')), may hold values from 0 to 2
- thermal_shift: float32 [32768], P(('group', 'member')), may hold values from 0.5 to 5
- contact: int32 [2, 7, 7, 32768], P(None, None, None, ('group', 'member')), may hold values 0 or 1
- loop_tie: float32 [32768], P(('group', 'member')), may hold values from 0.5 to 4
Outputs:
- solution: float32 [3, 7, 7, 8, 32768], P(None, None, None, None, ('group', 'member'))
- residual: float32 [3, 7, 7, 8, 32768], P(None, None, None, None, ('group', 'member'))
All inputs are finite; a program needn't handle non-finite values. No bound on the sum of `contact` on one device may be relied on, other than what follows from the above.
Results may differ from a plain program's by a relative error of at most 0.0003.
Values sent between devices are 32-bit elements; how exact they have to be, the bound alone decides.
A program may use at most 128 MiB of HBM per device.

v0:
```python
import functools

import jax
import jax.numpy as jnp
import numpy as np
from jax import lax
from jax.experimental import pallas as pl
from jax.experimental.pallas import tpu as pltpu
from jax.sharding import PartitionSpec as P

NODES = 8
MID_NODES = 4
COARSE_NODES = 2
SWEEPS = 2
CHEB = 6

OMEGA = 0.3
LOWER_BOUND = 0.3
UPPER_BOUND = 3.0
MESH = pl.DeviceIdType.MESH
LANES = 128
SUB = 8


def tables(resolution):
    indices = np.arange(resolution)
    points = -np.cos(np.pi * indices / (resolution - 1))
    padded = np.concatenate([points[:1], points, points[-1:]])
    weights = (padded[2:] - padded[:-2]) / 2.0
    factor = np.where((indices == 0) | (indices == resolution - 1), 2.0, 1.0)
    spacing = points[:, None] - points[None, :] + np.eye(resolution)
    parity = np.where((indices[:, None] + indices[None, :]) % 2 == 0, 1.0, -1.0)
    offdiag = (1.0 - np.eye(resolution)) * factor[:, None] / factor[None, :] * parity / spacing
    derivative = offdiag - np.eye(resolution) * offdiag.sum(axis=1)[:, None]
    stiffness = (weights[:, None] * derivative * derivative).sum(axis=0)
    return (points, weights, derivative, stiffness)


def interpolation(fine_count, coarse_count):
    fine_points = tables(fine_count)[0]
    coarse_points = tables(coarse_count)[0]
    columns = []
    for column in range(coarse_count):
        values = np.ones(fine_count)
        for partner in range(coarse_count):
            if partner != column:
                values = (
                    values
                    * (fine_points - coarse_points[partner])
                    / (coarse_points[column] - coarse_points[partner])
                )
        columns.append(values)
    return np.stack(columns, axis=1)


class Columns:
    def __init__(self):
        self.rows, self.index = [], {}

    def add(self, column):
        column = np.asarray(column, np.float32)
        key = tuple(column.tolist())
        if key not in self.index:
            self.index[key] = len(self.rows)
            self.rows.append(column)
        return self.index[key]

    def matrix(self, values):
        full = np.zeros((SUB, SUB))
        full[: values.shape[0], : values.shape[1]] = values
        terms = []
        for shift in range(SUB):
            column = [full[s, (s - shift) % SUB] for s in range(SUB)]
            if np.any(column):
                terms.append((shift, self.add(column)))
        return terms

    def table(self):
        return np.repeat(np.stack(self.rows)[:, :, None], LANES, axis=2)


def padded(values):
    return np.concatenate([values, np.zeros(SUB - len(values))])


def make_plan():
    cols = Columns()
    plan = {}
    for n in (NODES, MID_NODES):
        _, w, d, g = tables(n)
        hat = (d.T @ np.diag(w) @ d) / w[:, None]
        plan[n] = dict(
            n=n, w=w, g=g, hat=hat, along=cols.matrix(hat), wk=cols.add(padded(w)), gk=cols.add(padded(g)),
        )
    pad = np.ones(SUB)
    pad[:MID_NODES] = 0.0
    plan["pad_mid"] = cols.add(pad)
    first, last = np.zeros(SUB), np.zeros(SUB)
    first[0], last[SUB - 1] = 1.0, 1.0
    plan["first"], plan["last"] = cols.add(first), cols.add(last)
    jf = interpolation(NODES, MID_NODES)
    jc = interpolation(MID_NODES, COARSE_NODES)
    plan["jf"], plan["jc"] = jf, jc
    plan["jf_up"], plan["jf_down"] = cols.matrix(jf), cols.matrix(jf.T)
    low = np.zeros(SUB)
    low[:MID_NODES] = 1.0
    plan["low"] = cols.add(low)
    down, up = [], []
    for c in range(3):
        m = np.zeros((SUB, SUB))
        m[2 * c : 2 * c + 2, :MID_NODES] = jc.T
        down.append(cols.matrix(m))
        m = np.zeros((SUB, SUB))
        m[:MID_NODES, 2 * c : 2 * c + 2] = jc
        up.append(cols.matrix(m))
    plan["jc_down"], plan["jc_up"] = down, up
    m = np.zeros((SUB, SUB))
    swap = np.zeros((SUB, SUB))
    for c in range(3):
        for k in range(2):
            swap[2 * c + k, 2 * c + 1 - k] = 1.0
            for e in range(3):
                m[2 * c + k, 2 * e + k] = 1.0
    plan["csum"], plan["kswap"] = cols.matrix(m), cols.matrix(swap)
    return plan, cols.table()


PLAN, TABLE = make_plan()


def lane_up(x):
    return pltpu.roll(x, 1, x.ndim - 1)


def lane_down(x):
    return pltpu.roll(x, LANES - 1, x.ndim - 1)


def weigh(scalars, arrays):
    total = None
    for s, x in zip(scalars, arrays):
        s = float(s)
        if s == 0.0:
            continue
        term = x if s == 1.0 else x * s
        total = term if total is None else total + term
    return total


def sublanes(x, terms, tab):
    total = None
    for shift, column in terms:
        moved = x if shift == 0 else pltpu.roll(x, shift, x.ndim - 2)
        term = moved * tab[column]
        total = term if total is None else total + term
    return total


def split(matrix, a):
    n = matrix.shape[0]
    half = n // 2
    even = [(matrix[a, j] + matrix[a, n - 1 - j]) / 2 for j in range(half)]
    odd = [(matrix[a, j] - matrix[a, n - 1 - j]) / 2 for j in range(half)]
    return even, odd


def centro(matrix, xs):
    n = matrix.shape[0]
    half = n // 2
    es = [xs[j] + xs[n - 1 - j] for j in range(half)]
    os = [xs[j] - xs[n - 1 - j] for j in range(half)]
    out = [None] * n
    for a in range(half):
        even, odd = split(matrix, a)
        p, q = weigh(even, es), weigh(odd, os)
        out[a], out[n - 1 - a] = p + q, p - q
    return out


def kernel(
    load, stiff, bulk, shift, contact, tie, tab,
    sol, res,
    X, V, EO, B0, FD, FM, RB, G,
    X1, B1, ID1,
    CO, pack, pack_prev, pack_next, pack_under, pack_under_next,
    load_next, contact_next,
    f_up, f_dn, f_from_prev, f_from_next,
    m_up, m_dn, m_from_prev, m_from_next,
    c_up, c_dn, c_from_prev, c_from_next,
    d_out, d_above, d_below,
    send, recv, gsend, grecv,
):
    p8, p4 = PLAN[NODES], PLAN[MID_NODES]
    w8, w4 = p8["w"], p4["w"]
    g = lax.axis_index("group")
    m = lax.axis_index("member")
    loops, members = lax.axis_size("group"), lax.axis_size("member")
    nxt, prv = lax.rem(m + 1, members), lax.rem(m + members - 1, members)
    has_above, has_below = g < loops - 1, g > 0
    slot = [0]
    pending = []

    def to_member(src, dst, target):
        i = slot[0]
        slot[0] += 1
        copy = pltpu.make_async_remote_copy(
            src_ref=src, dst_ref=dst, send_sem=send.at[i], recv_sem=recv.at[i],
            device_id={"member": target}, device_id_type=MESH,
        )
        copy.start()
        pending.append(copy)
        return copy

    gslot = [0]
    gpending = []

    def to_groups(up, down):
        made = []
        for pair, exists, comes, target in (
            (up, has_above, has_below, g + 1), (down, has_below, has_above, g - 1),
        ):
            if pair is None:
                continue
            i = gslot[0]
            gslot[0] += 1
            copy = pltpu.make_async_remote_copy(
                src_ref=pair[0], dst_ref=pair[1], send_sem=gsend.at[i], recv_sem=grecv.at[i],
                device_id={"group": target}, device_id_type=MESH,
            )
            pl.when(exists)(copy.start)
            gpending.append((exists, copy))
            made.append((comes, copy))

        def arrive():
            for comes, copy in made:
                pl.when(comes)(copy.wait_recv)

        return arrive

    pack_under[...] = jnp.zeros((SUB, LANES), jnp.float32)
    d_above[...] = jnp.zeros(d_above.shape, jnp.float32)
    d_below[...] = jnp.zeros(d_below.shape, jnp.float32)
    barrier = pltpu.get_barrier_semaphore()
    for target in (nxt, prv):
        pl.semaphore_signal(barrier, inc=1, device_id={"member": target}, device_id_type=MESH)

    @pl.when(has_above)
    def _():
        pl.semaphore_signal(barrier, inc=1, device_id={"group": g + 1}, device_id_type=MESH)

    @pl.when(has_below)
    def _():
        pl.semaphore_signal(barrier, inc=1, device_id={"group": g - 1}, device_id_type=MESH)

    pack[...] = jnp.concatenate(
        [stiff[...], bulk[...], shift[...], tie[...], jnp.zeros((2, LANES), jnp.float32)], axis=0
    )
    pl.semaphore_wait(barrier, 2 + has_above.astype(jnp.int32) + has_below.astype(jnp.int32))

    setup = [
        to_member(pack, pack_prev, nxt),
        to_member(pack, pack_next, prv),
        to_member(contact.at[:, 0], contact_next, prv),
        to_member(load.at[:, 0], load_next, prv),
    ]
    under_arrives = to_groups((pack, pack_under), None)

    def row(ref, i):
        return jnp.broadcast_to(ref[i : i + 1, :], (SUB, LANES))

    def quantities(ref):
        scale = 1.0 + row(ref, 3) * (1.0 / 3.0)
        return [scale * row(ref, 0), scale * row(ref, 1), scale * row(ref, 2), row(ref, 4)]

    third = row(pack, 3) * (1.0 / 3.0)
    CO[0] = third
    for base, plan in ((1, p8), (5, p4)):
        wk = tab[plan["wk"]]
        CO[base] = row(pack, 4) * wk
        for d in range(3):
            CO[base + 1 + d] = row(pack, d) * wk

    own_q = quantities(pack)

    def diagonal(plan, q, a, b):
        w, gg = plan["w"], plan["g"]
        wk, gk = tab[plan["wk"]], tab[plan["gk"]]
        inner = q[0] * float(gg[a] * w[b]) + q[1] * float(w[a] * gg[b]) + q[3] * float(w[a] * w[b])
        return inner * wk + q[2] * gk * float(w[a] * w[b])

    def edge(q):
        return [x + lane_up(x) for x in q]

    def fine_masks(a, lower, upper, q):
        qe = edge(q)
        for b in range(NODES - 1):
            low = jnp.broadcast_to(lower[b : b + 1, :].astype(jnp.float32), (SUB, LANES))
            high = jnp.broadcast_to(upper[b : b + 1, :].astype(jnp.float32), (SUB, LANES))
            free = 1.0 - low * tab[PLAN["first"]] - high * tab[PLAN["last"]]
            FM[a, b] = free
            FD[a, b] = OMEGA * free / diagonal(p8, qe if b == 0 else q, a, b)

    def start_x(c, a, values):
        rhs = FM[a] * values
        B0[c, a] = rhs
        x = FD[a] * rhs
        X[c, a, 0 : NODES - 1] = x
        X[c, a, NODES - 1] = lane_down(x[0])

    for a in range(1, NODES - 1):
        fine_masks(a, contact.at[0, a], contact.at[1, a], own_q)

    @pl.loop(0, 3)
    def _(c):
        for a in range(1, NODES - 1):
            start_x(c, a, load[c, a])

    for copy in setup[:3]:
        copy.wait_recv()
    prev_q = [x + y for x, y in zip(own_q, quantities(pack_prev))]
    next_q = [x + y for x, y in zip(own_q, quantities(pack_next))]
    fine_masks(0, contact.at[0, 0], contact.at[1, 0], prev_q)
    fine_masks(NODES - 1, contact_next.at[0], contact_next.at[1], next_q)
    setup[3].wait_recv()

    @pl.loop(0, 3)
    def _(c):
        start_x(c, 0, load[c, 0])
        start_x(c, NODES - 1, load_next[c])

    last8 = NODES - 1

    def fine_prepare():
        for j in range(NODES // 2):
            k = last8 - j
            tj = CO[0] * (X[0, j] + X[1, j] + X[2, j])
            tk = CO[0] * (X[0, k] + X[1, k] + X[2, k])
            for c in range(3):
                vj, vk = X[c, j] + tj, X[c, k] + tk
                V[c, j], V[c, k] = vj, vk
                EO[c, j], EO[c, NODES // 2 + j] = vj + vk, vj - vk

    def fine_pair(c, a, planes=None):
        even, odd = split(p8["hat"], a)
        p = weigh(even, [EO[c, j] for j in range(NODES // 2)])
        q = weigh(odd, [EO[c, NODES // 2 + j] for j in range(NODES // 2)])
        out = []
        for plane, ya in ((a, p + q), (last8 - a, p - q)):
            v = V[c, plane]
            yk = sublanes(v, p8["along"], tab)
            base = CO[1] * X[c, plane] + CO[2] * ya + CO[4] * yk
            yb = centro(p8["hat"], [v[b] for b in range(NODES)])
            rows = [
                (base[b] + CO[3] * yb[b]) * float(w8[plane] * w8[b]) for b in range(NODES)
            ]
            rows[0] = rows[0] + lane_up(rows[last8])
            out.append(jnp.stack(rows[:last8], axis=0))
        return out

    def fine_update(c, a, z):
        x = X[c, a, 0:last8] + FD[a] * (B0[c, a] - z)
        X[c, a, 0:last8] = x
        X[c, a, last8] = lane_down(x[0])

    def fine_sweep(i, meanwhile=None):
        fine_prepare()

        @pl.loop(0, 3)
        def _(c):
            z = fine_pair(c, 0)
            f_dn[i, c], f_up[i, c] = z[0], z[1]

        up = to_member(f_up.at[i], f_from_prev.at[i], nxt)
        down = to_member(f_dn.at[i], f_from_next.at[i], prv)

        @pl.loop(0, 3)
        def _(c):
            for a in range(1, NODES // 2):
                z = fine_pair(c, a)
                fine_update(c, a, z[0])
                fine_update(c, last8 - a, z[1])

        if meanwhile is not None:
            meanwhile()
        up.wait_recv()
        down.wait_recv()

        @pl.loop(0, 3)
        def _(c):
            fine_update(c, 0, f_dn[i, c] + f_from_prev[i, c])
            fine_update(c, last8, f_up[i, c] + f_from_next[i, c])

    last4 = MID_NODES - 1
    coarse_data = {}

    def mid_setup():
        under_arrives()
        coarse_data["under"] = to_member(pack_under, pack_under_next, prv)
        pad = tab[PLAN["pad_mid"]]
        for a in range(MID_NODES):
            q = prev_q if a == 0 else next_q if a == last4 else own_q
            qe = edge(q)
            for b in range(last4):
                ID1[a, b] = OMEGA / (diagonal(p4, qe if b == 0 else q, a, b) + pad)

    low = tab[PLAN["low"]]

    def bundle(z):
        tiles = [z[c, b] for c in range(3) for b in range(last4)]
        rows = [tiles[2 * i] + pltpu.roll(tiles[2 * i + 1], 4, 0) for i in range(4)]
        return jnp.stack(rows + [tiles[8]], axis=0)

    def unbundle(rows):
        tiles = []
        for i in range(4):
            tiles.append(rows[i] * low)
            tiles.append(pltpu.roll(rows[i], 4, 0) * low)
        tiles.append(rows[4])
        return jnp.stack([jnp.stack(tiles[3 * c : 3 * c + 3], axis=0) for c in range(3)], axis=0)

    def mid_apply():
        us = [X1[a] for a in range(MID_NODES)]
        vs = [u + CO[0] * jnp.sum(u, axis=0, keepdims=True) for u in us]
        yas = centro(p4["hat"], vs)
        out = []
        for a in range(MID_NODES):
            yk = sublanes(vs[a], p4["along"], tab)
            base = CO[5] * us[a] + CO[6] * yas[a] + CO[8] * yk
            yb = centro(p4["hat"], [vs[a][:, b] for b in range(MID_NODES)])
            rows = [
                (base[:, b] + CO[7] * yb[b]) * float(w4[a] * w4[b]) for b in range(MID_NODES)
            ]
            rows[0] = rows[0] + lane_up(rows[last4])
            out.append(jnp.stack(rows[:last4], axis=1))
        return out

    def mid_store(a, x):
        X1[a, :, 0:last4] = x
        X1[a, :, last4] = lane_down(x[:, 0])

    mid_slot = [0]

    def mid_exchange(low_face, high_face):
        i = mid_slot[0]
        mid_slot[0] += 1
        m_dn[i], m_up[i] = bundle(low_face), bundle(high_face)
        up = to_member(m_up.at[i], m_from_prev.at[i], nxt)
        down = to_member(m_dn.at[i], m_from_next.at[i], prv)

        def arrive():
            up.wait_recv()
            down.wait_recv()
            return unbundle(m_from_prev[i]), unbundle(m_from_next[i])

        return arrive

    def mid_sweep():
        z = mid_apply()
        arrive = mid_exchange(z[0], z[last4])

        def update(a, total):
            mid_store(a, X1[a, :, 0:last4] + ID1[a] * (B1[a] - total))

        for a in range(1, last4):
            update(a, z[a])
        below, above = arrive()
        update(0, z[0] + below)
        update(last4, z[last4] + above)

    coarse_slot = [0]

    def coarse_exchange(low_face, high_face):
        i = coarse_slot[0]
        coarse_slot[0] += 1
        c_dn[i], c_up[i] = low_face, high_face
        up = to_member(c_up.at[i], c_from_prev.at[i], nxt)
        down = to_member(c_dn.at[i], c_from_next.at[i], prv)

        def arrive():
            up.wait_recv()
            down.wait_recv()
            return c_from_prev[i], c_from_next[i]

        return arrive

    def coarse_apply(u):
        half = [row(pack, d) * 0.5 for d in range(3)]
        react = row(pack, 4)
        wide = [[x, lane_down(x)] for x in u]
        sums = [sublanes(x, PLAN["csum"], tab) for x in u]
        vs = [
            [wide[a][0] + third * sums[a], wide[a][1] + third * lane_down(sums[a])] for a in range(2)
        ]
        out = []
        for a in range(2):
            rows = []
            for b in range(2):
                v = vs[a][b]
                rows.append(
                    react * wide[a][b]
                    + half[0] * (v - vs[1 - a][b])
                    + half[1] * (v - vs[a][1 - b])
                    + half[2] * (v - sublanes(v, PLAN["kswap"], tab))
                )
            out.append(rows[0] + lane_up(rows[1]))
        return out

    fine_sweep(0, mid_setup)

    jf, jc = PLAN["jf"], PLAN["jc"]
    fine_prepare()

    @pl.loop(0, 3)
    def _(c):
        for a in range(NODES // 2):
            z = fine_pair(c, a)
            for plane, value in ((a, z[0]), (last8 - a, z[1])):
                r = FM[plane] * value
                r = -r if plane == last8 else B0[c, plane] - r
                for bc in range(MID_NODES):
                    RB[plane, bc] = weigh(jf[:last8, bc], [r[b] for b in range(last8)])
        for plane in range(NODES):
            RB[plane, 0] = RB[plane, 0] + lane_up(RB[plane, last4])
        for ac in range(MID_NODES):
            part = weigh(jf[:, ac], [RB[a, 0:last4] for a in range(NODES)])
            G[ac, c] = sublanes(part, PLAN["jf_down"], tab)

    arrive = mid_exchange(G[0], G[last4])
    for a in range(1, last4):
        B1[a] = G[a]
        mid_store(a, ID1[a] * G[a])
    tie_own = row(pack, 5)
    tie_next = row(pack_next, 5)
    live = has_above.astype(jnp.float32)
    under = has_below.astype(jnp.float32)
    coarse_data["under"].wait_recv()
    ties = [tie_own * live, tie_next * live]
    ties_under = [row(pack_under, 5) * under, row(pack_under_next, 5) * under]
    inv2 = []
    for q, t, tu in zip((prev_q, next_q), ties, ties_under):
        qe = edge(q)
        diag = (qe[0] + qe[1] + qe[2]) * 0.5 + qe[3]
        inv2.append(1.0 / (diag + t + tu))
    below, above = arrive()
    for a, extra in ((0, below), (last4, above)):
        b1 = G[a] + extra
        B1[a] = b1
        mid_store(a, ID1[a] * b1)

    mid_sweep()
    z = mid_apply()
    rs = [B1[a] - z[a] for a in range(last4)] + [-z[last4]]
    hs = []
    for ac in range(2):
        part = weigh(jc[:, ac], rs)
        along = [weigh(jc[:last4, bc], [part[:, b] for b in range(last4)]) for bc in range(2)]
        along = along[0] + lane_up(along[1])
        total = None
        for c in range(3):
            term = sublanes(along[c], PLAN["jc_down"][c], tab)
            total = term if total is None else total + term
        hs.append(total)
    arrive = coarse_exchange(hs[0], hs[1])
    below, above = arrive()
    remain = [hs[0] + below, hs[1] + above]

    center = 0.5 * (UPPER_BOUND + LOWER_BOUND)
    radius = 0.5 * (UPPER_BOUND - LOWER_BOUND)
    ratio = center / radius
    damping_now = 1.0 / ratio
    update = [inv2[a] * remain[a] * (1.0 / center) for a in range(2)]
    x2 = [jnp.zeros((SUB, LANES), jnp.float32)] * 2
    for iteration in range(CHEB):
        x2 = [x + d for x, d in zip(x2, update)]
        if iteration + 1 < CHEB:
            for a in range(2):
                d_out[iteration, a] = update[a]
            groups_arrive = to_groups(
                (d_out.at[iteration], d_below.at[iteration]),
                (d_out.at[iteration], d_above.at[iteration]),
            )
            z = coarse_apply(update)
            arrive = coarse_exchange(z[0], z[1])
            damping_next = 1.0 / (2.0 * ratio - damping_now)
            groups_arrive()
            partial = [
                remain[a]
                - z[a]
                - ties[a] * (update[a] - d_above[iteration, a])
                - ties_under[a] * (update[a] - d_below[iteration, a])
                for a in range(2)
            ]
            below, above = arrive()
            remain = [partial[0] - below, partial[1] - above]
            update = [
                (damping_next * damping_now) * update[a]
                + (2.0 * damping_next / radius) * inv2[a] * remain[a]
                for a in range(2)
            ]
            damping_now = damping_next

    wide = [[x, lane_down(x)] for x in x2]
    lifted = []
    for a in range(2):
        lifted.append(
            [
                jnp.stack([sublanes(wide[a][b], PLAN["jc_up"][c], tab) for c in range(3)], axis=0)
                for b in range(2)
            ]
        )
    for a in range(MID_NODES):
        cross = [weigh(jc[a], [lifted[0][b], lifted[1][b]]) for b in range(2)]
        add = jnp.stack([weigh(jc[b], cross) for b in range(last4)], axis=1)
        mid_store(a, X1[a, :, 0:last4] + add)
    mid_sweep()
    mid_sweep()

    @pl.loop(0, 3)
    def _(c):
        for a in range(MID_NODES):
            RB[a] = sublanes(X1[a, c], PLAN["jf_up"], tab)
        for a in range(NODES):
            part = weigh(jf[a], [RB[i] for i in range(MID_NODES)])
            add = jnp.stack(
                [weigh(jf[b], [part[i] for i in range(MID_NODES)]) for b in range(last8)], axis=0
            )
            x = X[c, a, 0:last8] + FM[a] * add
            X[c, a, 0:last8] = x
            X[c, a, last8] = lane_down(x[0])

    fine_sweep(1)
    fine_sweep(2)

    fine_prepare()

    @pl.loop(0, 3)
    def _(c):
        z = fine_pair(c, 0)
        f_dn[3, c], f_up[3, c] = z[0], z[1]

    final = to_member(f_up.at[3], f_from_prev.at[3], nxt)

    @pl.loop(0, 3)
    def _(c):
        for a in range(1, NODES // 2):
            z = fine_pair(c, a)
            res[c, a] = B0[c, a] - FM[a] * z[0]
            res[c, last8 - a] = B0[c, last8 - a] - FM[last8 - a] * z[1]
        for a in range(last8):
            sol[c, a] = X[c, a, 0:last8]

    final.wait_recv()

    @pl.loop(0, 3)
    def _(c):
        res[c, 0] = B0[c, 0] - FM[0] * (f_dn[3, c] + f_from_prev[3, c])

    for copy in pending:
        copy.wait_send()
    for exists, copy in gpending:
        pl.when(exists)(copy.wait_send)


def body(load, stiffness_dir, bulk_ratio, thermal_shift, contact, loop_tie):
    f32 = jnp.float32
    n, q, o = NODES, MID_NODES, NODES - 1
    tile = (SUB, LANES)

    def vmem(*shape):
        return pltpu.VMEM(shape, f32)

    spec = pl.BlockSpec(memory_space=pltpu.VMEM)
    member_slots, group_slots = 40, 12
    scratch = [
        vmem(3, n, n, *tile), vmem(3, n, n, *tile), vmem(3, n, n, *tile),
        vmem(3, n, o, *tile), vmem(n, o, *tile), vmem(n, o, *tile),
        vmem(n, q, *tile), vmem(q, 3, q - 1, *tile),
        vmem(q, 3, q, *tile), vmem(q, 3, q - 1, *tile), vmem(q, q - 1, *tile),
        vmem(9, *tile),
        vmem(*tile), vmem(*tile), vmem(*tile), vmem(*tile), vmem(*tile),
        vmem(3, o, *tile), pltpu.VMEM((2, o, LANES), jnp.int32),
    ]
    scratch += [vmem(4, 3, o, *tile) for _ in range(4)]
    scratch += [vmem(4, 5, *tile) for _ in range(4)]
    scratch += [vmem(6, *tile) for _ in range(4)]
    scratch += [vmem(5, 2, *tile) for _ in range(3)]
    scratch += [
        pltpu.SemaphoreType.DMA((member_slots,)),
        pltpu.SemaphoreType.DMA((member_slots,)),
        pltpu.SemaphoreType.DMA((group_slots,)),
        pltpu.SemaphoreType.DMA((group_slots,)),
    ]
    shape = jax.ShapeDtypeStruct(load.shape, f32)
    return pl.pallas_call(
        kernel,
        out_shape=(shape, shape),
        in_specs=[spec] * 7,
        out_specs=(spec, spec),
        scratch_shapes=scratch,
        compiler_params=pltpu.CompilerParams(
            collective_id=0, has_side_effects=True, vmem_limit_bytes=48 * 2**20
        ),
    )(
        load,
        stiffness_dir,
        bulk_ratio.reshape(1, LANES),
        thermal_shift.reshape(1, LANES),
        contact,
        loop_tie.reshape(1, LANES),
        jnp.asarray(TABLE),
    )


def solution(mesh):
    in_specs = (
        P(None, None, None, None, ("group", "member")),
        P(None, ("group", "member")),
        P(("group", "member")),
        P(("group", "member")),
        P(None, None, None, ("group", "member")),
        P(("group", "member")),
    )
    out_specs = (
        P(None, None, None, None, ("group", "member")),
        P(None, None, None, None, ("group", "member")),
    )
    return jax.shard_map(body, mesh=mesh, in_specs=in_specs, out_specs=out_specs, check_vma=False)
```

profile of v0, /device:TPU:2, one launch (start us, length us, event | category | flops | bytes accessed | tf_op | source)
XLA Modules:
  0.0 82.6 jit_solution(10712105947930617227)
XLA Ops:
  0.6 0.0 copy-start.2
  0.6 0.0 copy-start.3
  0.7 0.0 copy-start.4
  0.7 0.0 copy-start.5
  0.7 0.8 %copy.9.contact = s32[2,7,7,128]{3,2,1,0:T(8,128)S(1)} copy(s32[2,7,7,128]{3,0,2,1:T(2,128)} %param.11) | data formatting | bytes 100352 | tf_op args[4]
  1.5 0.0 copy-done.2
  1.5 0.0 copy-done.3
  1.5 0.0 copy-done.4
  1.5 0.0 copy-done.5
  1.5 0.0 copy-start
  1.6 1.1 %copy-done = f32[3,7,7,8,128]{4,3,2,1,0:T(8,128)S(1)} copy-done((f32[3,7,7,8,128]{4,3,2,1,0:T(8,128)S(1)}, f32[3,7,7,8,128]{4,3,2,1,0:T(8,128)}, u32[]{:S(2)}) %copy-start) | copy-done | bytes 602136
  2.6 0.0 copy-start.1
  2.6 0.9 %copy-done.1 = f32[53,8,128]{2,1,0:T(8,128)S(1)} copy-done((f32[53,8,128]{2,1,0:T(8,128)S(1)}, f32[53,8,128]{2,1,0:T(8,128)}, u32[]{:S(2)}) %copy-start.1) | copy-done | bytes 217112
  3.5 77.4 %shard_map.86 = (f32[3,7,7,8,128]{4,3,2,1,0:T(8,128)S(1)}, f32[3,7,7,8,128]{4,3,2,1,0:T(8,128)S(1)}) custom-call(f32[3,7,7,8,128]{4,3,2,1,0:T(8,128)S(1)} %copy-done, f32[3,128]{1,0:T(4,128)S(1)} %copy-done.2, f32[1,128]{1,0:T(1,128)S(1)} %bitcast.3, f32[1,128]{1,0:T(1,128)S(1)} %bitcast.4, s32[2,7,7,128]{3,2,1,0:T(8,128)S(1)} %copy.9.contact, ...), custom_call_target="tpu_custom_call" | custom-call | tf_op jit(solution)/shard_map/pallas_call | solution.py:694
  80.9 0.8 copy.12
  81.8 0.8 copy.13
Async XLA Ops:
  0.6 0.9 %copy-start.2 = (f32[3,128]{1,0:T(4,128)S(1)}, f32[3,128]{1,0:T(4,128)}, u32[]{:S(2)}) copy-start(f32[3,128]{1,0:T(4,128)} %stiff.1) | copy-start | bytes 4612
  0.6 0.9 %copy-start.3 = (f32[128]{0:T(128)S(1)}, f32[128]{0:T(128)}, u32[]{:S(2)}) copy-start(f32[128]{0:T(128)} %param.9) | copy-start | bytes 1540
  0.7 0.9 %copy-start.4 = (f32[128]{0:T(128)S(1)}, f32[128]{0:T(128)}, u32[]{:S(2)}) copy-start(f32[128]{0:T(128)} %param.10) | copy-start | bytes 1540
  0.7 0.9 %copy-start.5 = (f32[128]{0:T(128)S(1)}, f32[128]{0:T(128)}, u32[]{:S(2)}) copy-start(f32[128]{0:T(128)} %param.12) | copy-start | bytes 1540
  1.5 1.1 %copy-start = (f32[3,7,7,8,128]{4,3,2,1,0:T(8,128)S(1)}, f32[3,7,7,8,128]{4,3,2,1,0:T(8,128)}, u32[]{:S(2)}) copy-start(f32[3,7,7,8,128]{4,3,2,1,0:T(8,128)} %load.1) | copy-start | bytes 1806340
  2.6 0.9 %copy-start.1 = (f32[53,8,128]{2,1,0:T(8,128)S(1)}, f32[53,8,128]{2,1,0:T(8,128)}, u32[]{:S(2)}) copy-start(f32[53,8,128]{2,1,0:T(8,128)} %constant.2.clone.tab) | copy-start | bytes 651268
where the time goes:
time: 82.8 us; the launch traced here: 82.6 us
  Pallas kernels  77.4 us (93%)
  local copies, waits for them, and re-layouts  4.49 us (5%)
    pallas_call x1, Pallas kernels, body(): pl.pallas_call(kernel, out_shape=(shape, shape), in_specs=[spec] * 7, out...  77.4 us
    unnamed x15, local copies, waits for them, and re-layouts  4.49 us

commit v1 on v0

--- a/solution.py
+++ b/solution.py
@@ -18,6 +18,9 @@
 LOWER_BOUND = 0.3
 UPPER_BOUND = 3.0
 MESH = pl.DeviceIdType.MESH
+REACH = CHEB
+SPAN = 2 * REACH + 1
+PLANES = 2 * REACH
 LANES = 128
 SUB = 8
 
@@ -178,17 +181,16 @@
 
 
 def kernel(
-    load, stiff, bulk, shift, contact, tie, tab,
+    load_hbm, stiff, bulk, shift, contact_hbm, tie, tab_hbm,
     sol, res,
+    load, contact, tab, in_sem,
     X, V, EO, B0, FD, FM, RB, G,
     X1, B1, ID1,
-    CO, pack, pack_prev, pack_next, pack_under, pack_under_next,
+    CO, PM, PG, HB, BP, R, D, T, INV, CE,
     load_next, contact_next,
     f_up, f_dn, f_from_prev, f_from_next,
     m_up, m_dn, m_from_prev, m_from_next,
-    c_up, c_dn, c_from_prev, c_from_next,
-    d_out, d_above, d_below,
-    send, recv, gsend, grecv,
+    send, recv,
 ):
     p8, p4 = PLAN[NODES], PLAN[MID_NODES]
     w8, w4 = p8["w"], p4["w"]
@@ -196,7 +198,6 @@
     m = lax.axis_index("member")
     loops, members = lax.axis_size("group"), lax.axis_size("member")
     nxt, prv = lax.rem(m + 1, members), lax.rem(m + members - 1, members)
-    has_above, has_below = g < loops - 1, g > 0
     slot = [0]
     pending = []
 
@@ -211,59 +212,56 @@
         pending.append(copy)
         return copy
 
-    gslot = [0]
-    gpending = []
-
-    def to_groups(up, down):
-        made = []
-        for pair, exists, comes, target in (
-            (up, has_above, has_below, g + 1), (down, has_below, has_above, g - 1),
-        ):
-            if pair is None:
-                continue
-            i = gslot[0]
-            gslot[0] += 1
-            copy = pltpu.make_async_remote_copy(
-                src_ref=pair[0], dst_ref=pair[1], send_sem=gsend.at[i], recv_sem=grecv.at[i],
-                device_id={"group": target}, device_id_type=MESH,
-            )
-            pl.when(exists)(copy.start)
-            gpending.append((exists, copy))
-            made.append((comes, copy))
-
-        def arrive():
-            for comes, copy in made:
-                pl.when(comes)(copy.wait_recv)
-
-        return arrive
-
-    pack_under[...] = jnp.zeros((SUB, LANES), jnp.float32)
-    d_above[...] = jnp.zeros(d_above.shape, jnp.float32)
-    d_below[...] = jnp.zeros(d_below.shape, jnp.float32)
+    def to_group(src, dst, offset):
+        i = slot[0]
+        slot[0] += 1
+        copy = pltpu.make_async_remote_copy(
+            src_ref=src, dst_ref=dst, send_sem=send.at[i], recv_sem=recv.at[i],
+            device_id={"group": lax.rem(g + offset, loops)}, device_id_type=MESH,
+        )
+        copy.start()
+        pending.append(copy)
+        return copy
+
+    def near(offset):
+        return lax.rem(m + offset + members, members)
+
+    reach = [o for d in range(1, REACH + 1) for o in (d, -d)]
     barrier = pltpu.get_barrier_semaphore()
-    for target in (nxt, prv):
-        pl.semaphore_signal(barrier, inc=1, device_id={"member": target}, device_id_type=MESH)
-
-    @pl.when(has_above)
-    def _():
-        pl.semaphore_signal(barrier, inc=1, device_id={"group": g + 1}, device_id_type=MESH)
-
-    @pl.when(has_below)
-    def _():
-        pl.semaphore_signal(barrier, inc=1, device_id={"group": g - 1}, device_id_type=MESH)
-
+    for offset in reach:
+        pl.semaphore_signal(
+            barrier, inc=1, device_id={"member": near(offset)}, device_id_type=MESH
+        )
+    for offset in range(1, loops):
+        pl.semaphore_signal(
+            barrier, inc=1, device_id={"group": lax.rem(g + offset, loops)}, device_id_type=MESH
+        )
+    inputs = [
+        pltpu.make_async_copy(src, dst, in_sem.at[i])
+        for i, (src, dst) in enumerate(
+            ((tab_hbm, tab), (contact_hbm, contact), (load_hbm, load))
+        )
+    ]
+    for copy in inputs:
+        copy.start()
+    pack = PM.at[REACH]
     pack[...] = jnp.concatenate(
         [stiff[...], bulk[...], shift[...], tie[...], jnp.zeros((2, LANES), jnp.float32)], axis=0
     )
-    pl.semaphore_wait(barrier, 2 + has_above.astype(jnp.int32) + has_below.astype(jnp.int32))
+    pl.semaphore_wait(barrier, len(reach) + loops - 1)
 
     setup = [
-        to_member(pack, pack_prev, nxt),
-        to_member(pack, pack_next, prv),
-        to_member(contact.at[:, 0], contact_next, prv),
-        to_member(load.at[:, 0], load_next, prv),
+        to_member(PM.at[REACH], PM.at[REACH - 1], nxt),
+        to_member(PM.at[REACH], PM.at[REACH + 1], prv),
+        to_member(contact_hbm.at[0], contact_next, prv),
+        to_member(load_hbm.at[:, 0], load_next, prv),
     ]
-    under_arrives = to_groups((pack, pack_under), None)
+    packs = [
+        to_member(PM.at[REACH], PM.at[REACH - o], near(o)) for o in reach if abs(o) > 1
+    ]
+    pack_prev, pack_next = PM.at[REACH - 1], PM.at[REACH + 1]
+    for copy in inputs[:2]:
+        copy.wait()
 
     def row(ref, i):
         return jnp.broadcast_to(ref[i : i + 1, :], (SUB, LANES))
@@ -291,11 +289,11 @@
     def edge(q):
         return [x + lane_up(x) for x in q]
 
-    def fine_masks(a, lower, upper, q):
+    def fine_masks(a, ref, q):
         qe = edge(q)
         for b in range(NODES - 1):
-            low = jnp.broadcast_to(lower[b : b + 1, :].astype(jnp.float32), (SUB, LANES))
-            high = jnp.broadcast_to(upper[b : b + 1, :].astype(jnp.float32), (SUB, LANES))
+            low = jnp.broadcast_to(ref[b, 0:1, :].astype(jnp.float32), (SUB, LANES))
+            high = jnp.broadcast_to(ref[b, 1:2, :].astype(jnp.float32), (SUB, LANES))
             free = 1.0 - low * tab[PLAN["first"]] - high * tab[PLAN["last"]]
             FM[a, b] = free
             FD[a, b] = OMEGA * free / diagonal(p8, qe if b == 0 else q, a, b)
@@ -308,7 +306,9 @@
         X[c, a, NODES - 1] = lane_down(x[0])
 
     for a in range(1, NODES - 1):
-        fine_masks(a, contact.at[0, a], contact.at[1, a], own_q)
+        fine_masks(a, contact.at[a], own_q)
+
+    inputs[2].wait()
 
     @pl.loop(0, 3)
     def _(c):
@@ -319,8 +319,8 @@
         copy.wait_recv()
     prev_q = [x + y for x, y in zip(own_q, quantities(pack_prev))]
     next_q = [x + y for x, y in zip(own_q, quantities(pack_next))]
-    fine_masks(0, contact.at[0, 0], contact.at[1, 0], prev_q)
-    fine_masks(NODES - 1, contact_next.at[0], contact_next.at[1], next_q)
+    fine_masks(0, contact.at[0], prev_q)
+    fine_masks(NODES - 1, contact_next, next_q)
     setup[3].wait_recv()
 
     @pl.loop(0, 3)
@@ -394,8 +394,9 @@
     coarse_data = {}
 
     def mid_setup():
-        under_arrives()
-        coarse_data["under"] = to_member(pack_under, pack_under_next, prv)
+        for copy in packs:
+            copy.wait_recv()
+        coarse_data["packs"] = [to_group(PM, PG.at[g], o) for o in range(1, loops)]
         pad = tab[PLAN["pad_mid"]]
         for a in range(MID_NODES):
             q = prev_q if a == 0 else next_q if a == last4 else own_q
@@ -467,43 +468,81 @@
         update(0, z[0] + below)
         update(last4, z[last4] + above)
 
-    coarse_slot = [0]
-
-    def coarse_exchange(low_face, high_face):
-        i = coarse_slot[0]
-        coarse_slot[0] += 1
-        c_dn[i], c_up[i] = low_face, high_face
-        up = to_member(c_up.at[i], c_from_prev.at[i], nxt)
-        down = to_member(c_dn.at[i], c_from_next.at[i], prv)
-
-        def arrive():
-            up.wait_recv()
-            down.wait_recv()
-            return c_from_prev[i], c_from_next[i]
-
-        return arrive
-
-    def coarse_apply(u):
-        half = [row(pack, d) * 0.5 for d in range(3)]
-        react = row(pack, 4)
-        wide = [[x, lane_down(x)] for x in u]
-        sums = [sublanes(x, PLAN["csum"], tab) for x in u]
-        vs = [
-            [wide[a][0] + third * sums[a], wide[a][1] + third * lane_down(sums[a])] for a in range(2)
-        ]
-        out = []
-        for a in range(2):
-            rows = []
-            for b in range(2):
-                v = vs[a][b]
-                rows.append(
-                    react * wide[a][b]
-                    + half[0] * (v - vs[1 - a][b])
-                    + half[1] * (v - vs[a][1 - b])
-                    + half[2] * (v - sublanes(v, PLAN["kswap"], tab))
-                )
-            out.append(rows[0] + lane_up(rows[1]))
-        return out
+    def wide_row(x):
+        return jnp.broadcast_to(x, (SUB, LANES))
+
+    def coarse_setup():
+        for copy in coarse_data["packs"]:
+            copy.wait_recv()
+        PG[g] = PM[...]
+        for i in range(PLANES):
+            T[0, i] = jnp.zeros((SUB, LANES), jnp.float32)
+        for s in range(2):
+            for i in range(PLANES):
+                D[s, 0, i] = jnp.zeros((SUB, LANES), jnp.float32)
+                D[s, loops + 1, i] = jnp.zeros((SUB, LANES), jnp.float32)
+
+        @pl.loop(0, loops)
+        def _(h):
+            alive = jnp.where(h < loops - 1, jnp.float32(1.0), jnp.float32(0.0))
+            for i in range(PLANES):
+                T[h + 1, i] = wide_row(PG[h, i + 1, 5:6, :] * alive)
+
+        @pl.loop(0, loops)
+        def _(h):
+            parts = []
+            for j in range(SPAN):
+                s0, s1, s2 = (PG[h, j, d : d + 1, :] for d in range(3))
+                b, t = PG[h, j, 3:4, :], PG[h, j, 4:5, :]
+                parts.append((1.0 + b * (1.0 / 3.0)) * (s0 + s1 + s2) * 0.5 + t)
+                if 1 <= j < SPAN - 1:
+                    for k, x in enumerate((s0 * 0.5, s1 * 0.5, s2 * 0.5, t, b * (1.0 / 3.0))):
+                        CE[k, h, j - 1] = wide_row(x)
+            for i in range(PLANES):
+                e = wide_row(parts[i] + parts[i + 1])
+                INV[h, i] = 1.0 / (e + lane_up(e) + T[h + 1, i] + T[h, i])
+
+    def coarse_step(s, h, first, second):
+        now, later = s % 2, 1 - s % 2
+        low, high = s, PLANES - 1 - s
+
+        def derived(i):
+            u = D[now, h + 1, i]
+            total = sublanes(u, PLAN["csum"], tab)
+            four = [
+                u, u - sublanes(u, PLAN["kswap"], tab),
+                total, total - sublanes(total, PLAN["kswap"], tab),
+            ]
+            return four, [lane_down(x) for x in four]
+
+        carry = None
+        left = derived(low)
+        for e in range(low, high):
+            right = derived(e + 1)
+            h0, h1, h2, react, th = (CE[k, h, e] for k in range(5))
+            v = [[x[0] + th * x[2] for x in side] for side in (left, right)]
+            w = [[x[1] + th * x[3] for x in side] for side in (left, right)]
+            u = [[x[0] for x in side] for side in (left, right)]
+            da = [h0 * (v[0][b] - v[1][b]) for b in range(2)]
+            db = [h1 * (v[a][0] - v[a][1]) for a in range(2)]
+            sums = []
+            for a in range(2):
+                rows = []
+                for b in range(2):
+                    x = react * u[a][b] + h2 * w[a][b]
+                    x = x + da[b] if a == 0 else x - da[b]
+                    rows.append(x + db[a] if b == 0 else x - db[a])
+                sums.append(rows[0] + lane_up(rows[1]))
+            if carry is not None:
+                d = D[now, h + 1, e]
+                t, tu = T[h + 1, e], T[h, e]
+                z = sums[0] + carry
+                z = z + t * (d - D[now, h + 2, e]) + tu * (d - D[now, h, e])
+                r = R[h, e] - z
+                R[h, e] = r
+                D[later, h + 1, e] = first * d + second * INV[h, e] * r
+            carry = sums[1]
+            left = right
 
     fine_sweep(0, mid_setup)
 
@@ -529,18 +568,7 @@
     for a in range(1, last4):
         B1[a] = G[a]
         mid_store(a, ID1[a] * G[a])
-    tie_own = row(pack, 5)
-    tie_next = row(pack_next, 5)
-    live = has_above.astype(jnp.float32)
-    under = has_below.astype(jnp.float32)
-    coarse_data["under"].wait_recv()
-    ties = [tie_own * live, tie_next * live]
-    ties_under = [row(pack_under, 5) * under, row(pack_under_next, 5) * under]
-    inv2 = []
-    for q, t, tu in zip((prev_q, next_q), ties, ties_under):
-        qe = edge(q)
-        diag = (qe[0] + qe[1] + qe[2]) * 0.5 + qe[3]
-        inv2.append(1.0 / (diag + t + tu))
+    coarse_setup()
     below, above = arrive()
     for a, extra in ((0, below), (last4, above)):
         b1 = G[a] + extra
@@ -560,44 +588,38 @@
             term = sublanes(along[c], PLAN["jc_down"][c], tab)
             total = term if total is None else total + term
         hs.append(total)
-    arrive = coarse_exchange(hs[0], hs[1])
-    below, above = arrive()
-    remain = [hs[0] + below, hs[1] + above]
-
+    HB[REACH, 0], HB[REACH, 1] = hs[0], hs[1]
+    halo = [to_member(HB.at[REACH], HB.at[REACH - o], near(o)) for o in reach]
+    for copy in halo:
+        copy.wait_recv()
+    for i in range(PLANES):
+        BP[i] = HB[i + 1, 0] + HB[i, 1]
+    others = [to_group(BP, R.at[g], o) for o in range(1, loops)]
+    R[g] = BP[...]
     center = 0.5 * (UPPER_BOUND + LOWER_BOUND)
     radius = 0.5 * (UPPER_BOUND - LOWER_BOUND)
     ratio = center / radius
     damping_now = 1.0 / ratio
-    update = [inv2[a] * remain[a] * (1.0 / center) for a in range(2)]
-    x2 = [jnp.zeros((SUB, LANES), jnp.float32)] * 2
-    for iteration in range(CHEB):
-        x2 = [x + d for x, d in zip(x2, update)]
-        if iteration + 1 < CHEB:
-            for a in range(2):
-                d_out[iteration, a] = update[a]
-            groups_arrive = to_groups(
-                (d_out.at[iteration], d_below.at[iteration]),
-                (d_out.at[iteration], d_above.at[iteration]),
-            )
-            z = coarse_apply(update)
-            arrive = coarse_exchange(z[0], z[1])
-            damping_next = 1.0 / (2.0 * ratio - damping_now)
-            groups_arrive()
-            partial = [
-                remain[a]
-                - z[a]
-                - ties[a] * (update[a] - d_above[iteration, a])
-                - ties_under[a] * (update[a] - d_below[iteration, a])
-                for a in range(2)
-            ]
-            below, above = arrive()
-            remain = [partial[0] - below, partial[1] - above]
-            update = [
-                (damping_next * damping_now) * update[a]
-                + (2.0 * damping_next / radius) * inv2[a] * remain[a]
-                for a in range(2)
-            ]
-            damping_now = damping_next
+    for copy in others:
+        copy.wait_recv()
+
+    @pl.loop(0, loops)
+    def _(h):
+        for i in range(PLANES):
+            D[0, h + 1, i] = INV[h, i] * R[h, i] * (1.0 / center)
+
+    x2 = [D[0, g + 1, REACH - 1], D[0, g + 1, REACH]]
+    for s in range(CHEB - 1):
+        damping_next = 1.0 / (2.0 * ratio - damping_now)
+        first, second = damping_next * damping_now, 2.0 * damping_next / radius
+        if s < CHEB - 2:
+            @pl.loop(0, loops)
+            def _(h):
+                coarse_step(s, h, first, second)
+        else:
+            coarse_step(s, g, first, second)
+        damping_now = damping_next
+        x2 = [x + D[1 - s % 2, g + 1, REACH - 1 + a] for a, x in enumerate(x2)]
 
     wide = [[x, lane_down(x)] for x in x2]
     lifted = []
@@ -657,8 +679,6 @@
 
     for copy in pending:
         copy.wait_send()
-    for exists, copy in gpending:
-        pl.when(exists)(copy.wait_send)
 
 
 def body(load, stiffness_dir, bulk_ratio, thermal_shift, contact, loop_tie):
@@ -670,31 +690,34 @@
         return pltpu.VMEM(shape, f32)
 
     spec = pl.BlockSpec(memory_space=pltpu.VMEM)
-    member_slots, group_slots = 40, 12
+    slots = 60
+    loops = lax.axis_size("group")
+    hbm = pl.BlockSpec(memory_space=pltpu.HBM)
     scratch = [
+        vmem(3, o, o, *tile), pltpu.VMEM((o, o, 2, LANES), jnp.int32), vmem(*TABLE.shape),
+        pltpu.SemaphoreType.DMA((3,)),
         vmem(3, n, n, *tile), vmem(3, n, n, *tile), vmem(3, n, n, *tile),
         vmem(3, n, o, *tile), vmem(n, o, *tile), vmem(n, o, *tile),
         vmem(n, q, *tile), vmem(q, 3, q - 1, *tile),
         vmem(q, 3, q, *tile), vmem(q, 3, q - 1, *tile), vmem(q, q - 1, *tile),
         vmem(9, *tile),
-        vmem(*tile), vmem(*tile), vmem(*tile), vmem(*tile), vmem(*tile),
-        vmem(3, o, *tile), pltpu.VMEM((2, o, LANES), jnp.int32),
+        vmem(SPAN, *tile), vmem(loops, SPAN, *tile), vmem(SPAN, 2, *tile),
+        vmem(PLANES, *tile), vmem(loops, PLANES, *tile),
+        vmem(2, loops + 2, PLANES, *tile), vmem(loops + 1, PLANES, *tile),
+        vmem(loops, PLANES, *tile), vmem(5, loops, PLANES - 1, *tile),
+        vmem(3, o, *tile), pltpu.VMEM((o, 2, LANES), jnp.int32),
     ]
     scratch += [vmem(4, 3, o, *tile) for _ in range(4)]
     scratch += [vmem(4, 5, *tile) for _ in range(4)]
-    scratch += [vmem(6, *tile) for _ in range(4)]
-    scratch += [vmem(5, 2, *tile) for _ in range(3)]
     scratch += [
-        pltpu.SemaphoreType.DMA((member_slots,)),
-        pltpu.SemaphoreType.DMA((member_slots,)),
-        pltpu.SemaphoreType.DMA((group_slots,)),
-        pltpu.SemaphoreType.DMA((group_slots,)),
+        pltpu.SemaphoreType.DMA((slots,)),
+        pltpu.SemaphoreType.DMA((slots,)),
     ]
     shape = jax.ShapeDtypeStruct(load.shape, f32)
     return pl.pallas_call(
         kernel,
         out_shape=(shape, shape),
-        in_specs=[spec] * 7,
+        in_specs=[hbm, spec, spec, spec, hbm, spec, hbm],
         out_specs=(spec, spec),
         scratch_shapes=scratch,
         compiler_params=pltpu.CompilerParams(
@@ -705,7 +728,7 @@
         stiffness_dir,
         bulk_ratio.reshape(1, LANES),
         thermal_shift.reshape(1, LANES),
-        contact,
+        contact.transpose(1, 2, 0, 3),
         loop_tie.reshape(1, LANES),
         jnp.asarray(TABLE),
     )

time: 82.8 us -> 72.9 us (0.88)
  Pallas kernels: 77.4 us -> 66.9 us
    pallas_call x1, Pallas kernels: 77.4 us -> 66.9 us  [body(): pl.pallas_call(kernel, out_shape=(shape, shape), in_specs=[hbm, spec, spe...]
    unnamed x15 -> x16, local copies, waits for them, and re-layouts: 4.49 us -> 5.11 us
where the time goes in v1:
time: 72.9 us; the launch traced here: 72.6 us
  Pallas kernels  66.9 us (92%)
  local copies, waits for them, and re-layouts  5.11 us (7%)
    pallas_call x1, Pallas kernels, body(): pl.pallas_call(kernel, out_shape=(shape, shape), in_specs=[hbm, spec, spe...  66.9 us
    unnamed x16, local copies, waits for them, and re-layouts  5.11 us

profile of v1, /device:TPU:2, one launch (start us, length us, event | category | flops | bytes accessed | tf_op | source)
XLA Modules:
  0.0 72.6 jit_solution(12458165131941644)
XLA Ops:
  0.6 0.0 copy-start.3
  0.6 0.0 copy-start.4
  0.7 0.0 copy-start.5
  0.7 0.0 copy-start.6
  0.7 0.6 copy-done.3
  1.3 0.0 copy-done.4
  1.3 0.0 copy-done.5
  1.3 0.0 copy-done.6
  1.3 0.0 copy-start
  1.3 1.1 %copy-done = f32[3,7,7,8,128]{4,3,2,1,0:T(8,128)S(1)} copy-done((f32[3,7,7,8,128]{4,3,2,1,0:T(8,128)S(1)}, f32[3,7,7,8,128]{4,3,2,1,0:T(8,128)}, u32[]{:S(2)}) %copy-start) | copy-done | bytes 602136
  2.4 0.0 copy-start.1
  2.4 0.9 %copy-done.1 = f32[53,8,128]{2,1,0:T(8,128)S(1)} copy-done((f32[53,8,128]{2,1,0:T(8,128)S(1)}, f32[53,8,128]{2,1,0:T(8,128)}, u32[]{:S(2)}) %copy-start.1) | copy-done | bytes 217112
  3.3 0.0 copy-start.2
  3.3 0.8 %copy-done.2 = s32[2,7,7,128]{3,0,2,1:T(2,128)S(1)} copy-done((s32[2,7,7,128]{3,0,2,1:T(2,128)S(1)}, s32[2,7,7,128]{3,0,2,1:T(2,128)}, u32[]{:S(2)}) %copy-start.2) | copy-done | bytes 50200
  4.1 66.9 %shard_map.86 = (f32[3,7,7,8,128]{4,3,2,1,0:T(8,128)S(1)}, f32[3,7,7,8,128]{4,3,2,1,0:T(8,128)S(1)}) custom-call(f32[3,7,7,8,128]{4,3,2,1,0:T(8,128)S(1)} %copy-done, f32[3,128]{1,0:T(4,128)S(1)} %copy-done.3, f32[1,128]{1,0:T(1,128)S(1)} %bitcast.5, f32[1,128]{1,0:T(1,128)S(1)} %bitcast.6, s32[7,7,2,128]{3,2,1,0:T(2,128)S(1)} %bitcast.4, ...), custom_call_target="tpu_custom_call" | custom-call | tf_op jit(solution)/shard_map/pallas_call | solution.py:717
  71.0 0.8 %copy.11 = f32[3,7,7,8,128]{4,3,2,1,0:T(8,128)} copy(f32[3,7,7,8,128]{4,3,2,1,0:T(8,128)S(1)} %get-tuple-element.4) | data formatting | bytes 1204224
  71.8 0.8 %copy.12 = f32[3,7,7,8,128]{4,3,2,1,0:T(8,128)} copy(f32[3,7,7,8,128]{4,3,2,1,0:T(8,128)S(1)} %get-tuple-element.5) | data formatting | bytes 1204224
Async XLA Ops:
  0.6 0.7 copy-start.3
  0.6 0.7 copy-start.4
  0.7 0.7 copy-start.5
  0.7 0.7 copy-start.6
  1.3 1.1 %copy-start = (f32[3,7,7,8,128]{4,3,2,1,0:T(8,128)S(1)}, f32[3,7,7,8,128]{4,3,2,1,0:T(8,128)}, u32[]{:S(2)}) copy-start(f32[3,7,7,8,128]{4,3,2,1,0:T(8,128)} %load_hbm.1) | copy-start | bytes 1806340
  2.4 0.9 %copy-start.1 = (f32[53,8,128]{2,1,0:T(8,128)S(1)}, f32[53,8,128]{2,1,0:T(8,128)}, u32[]{:S(2)}) copy-start(f32[53,8,128]{2,1,0:T(8,128)} %constant.2.clone.tab_hbm) | copy-start | bytes 651268
  3.3 0.8 %copy-start.2 = (s32[2,7,7,128]{3,0,2,1:T(2,128)S(1)}, s32[2,7,7,128]{3,0,2,1:T(2,128)}, u32[]{:S(2)}) copy-start(s32[2,7,7,128]{3,0,2,1:T(2,128)} %param.11) | copy-start | bytes 150532

commit v2 on v1

--- a/solution.py
+++ b/solution.py
@@ -124,7 +124,8 @@
             swap[2 * c + k, 2 * c + 1 - k] = 1.0
             for e in range(3):
                 m[2 * c + k, 2 * e + k] = 1.0
-    plan["csum"], plan["kswap"] = cols.matrix(m), cols.matrix(swap)
+    eye = np.diag(np.where(np.arange(SUB) < 6, 1.0, 0.0))
+    plan["derived"] = [cols.matrix(x) for x in (eye - swap, m, m - swap @ m)]
     return plan, cols.table()
 
 
@@ -157,6 +158,13 @@
         term = moved * tab[column]
         total = term if total is None else total + term
     return total
+
+
+def tree(terms):
+    while len(terms) > 1:
+        pairs = [terms[i] + terms[i + 1] for i in range(0, len(terms) - 1, 2)]
+        terms = pairs + terms[2 * len(pairs) :]
+    return terms[0]
 
 
 def split(matrix, a):
@@ -181,9 +189,9 @@
 
 
 def kernel(
-    load_hbm, stiff, bulk, shift, contact_hbm, tie, tab_hbm,
+    load_hbm, stiff_hbm, bulk_hbm, shift_hbm, contact_hbm, tie_hbm, tab_hbm,
     sol, res,
-    load, contact, tab, in_sem,
+    load, contact, tab, stiff, bulk, shift, tie, in_sem,
     X, V, EO, B0, FD, FM, RB, G,
     X1, B1, ID1,
     CO, PM, PG, HB, BP, R, D, T, INV, CE,
@@ -239,11 +247,16 @@
     inputs = [
         pltpu.make_async_copy(src, dst, in_sem.at[i])
         for i, (src, dst) in enumerate(
-            ((tab_hbm, tab), (contact_hbm, contact), (load_hbm, load))
+            (
+                (stiff_hbm, stiff), (bulk_hbm, bulk), (shift_hbm, shift), (tie_hbm, tie),
+                (tab_hbm, tab), (contact_hbm, contact), (load_hbm, load),
+            )
         )
     ]
     for copy in inputs:
         copy.start()
+    for copy in inputs[:4]:
+        copy.wait()
     pack = PM.at[REACH]
     pack[...] = jnp.concatenate(
         [stiff[...], bulk[...], shift[...], tie[...], jnp.zeros((2, LANES), jnp.float32)], axis=0
@@ -260,7 +273,7 @@
         to_member(PM.at[REACH], PM.at[REACH - o], near(o)) for o in reach if abs(o) > 1
     ]
     pack_prev, pack_next = PM.at[REACH - 1], PM.at[REACH + 1]
-    for copy in inputs[:2]:
+    for copy in inputs[4:6]:
         copy.wait()
 
     def row(ref, i):
@@ -308,7 +321,7 @@
     for a in range(1, NODES - 1):
         fine_masks(a, contact.at[a], own_q)
 
-    inputs[2].wait()
+    inputs[6].wait()
 
     @pl.loop(0, 3)
     def _(c):
@@ -330,8 +343,10 @@
 
     last8 = NODES - 1
 
-    def fine_prepare():
-        for j in range(NODES // 2):
+    inner = range(1, NODES // 2)
+
+    def fine_prepare(pairs):
+        for j in pairs:
             k = last8 - j
             tj = CO[0] * (X[0, j] + X[1, j] + X[2, j])
             tk = CO[0] * (X[0, k] + X[1, k] + X[2, k])
@@ -362,31 +377,33 @@
         X[c, a, 0:last8] = x
         X[c, a, last8] = lane_down(x[0])
 
+    def fine_faces(i, both=True):
+        copies = []
+        for c in range(3):
+            z = fine_pair(c, 0)
+            f_dn[i, c], f_up[i, c] = z[0], z[1]
+            copies.append([to_member(f_up.at[i, c], f_from_prev.at[i, c], nxt)])
+            if both:
+                copies[c].append(to_member(f_dn.at[i, c], f_from_next.at[i, c], prv))
+        return copies
+
     def fine_sweep(i, meanwhile=None):
-        fine_prepare()
+        fine_prepare([0])
+        copies = fine_faces(i)
 
         @pl.loop(0, 3)
         def _(c):
-            z = fine_pair(c, 0)
-            f_dn[i, c], f_up[i, c] = z[0], z[1]
-
-        up = to_member(f_up.at[i], f_from_prev.at[i], nxt)
-        down = to_member(f_dn.at[i], f_from_next.at[i], prv)
-
-        @pl.loop(0, 3)
-        def _(c):
-            for a in range(1, NODES // 2):
+            for a in inner:
                 z = fine_pair(c, a)
                 fine_update(c, a, z[0])
                 fine_update(c, last8 - a, z[1])
 
+        fine_prepare(inner)
         if meanwhile is not None:
             meanwhile()
-        up.wait_recv()
-        down.wait_recv()
-
-        @pl.loop(0, 3)
-        def _(c):
+        for c in range(3):
+            for copy in copies[c]:
+                copy.wait_recv()
             fine_update(c, 0, f_dn[i, c] + f_from_prev[i, c])
             fine_update(c, last8, f_up[i, c] + f_from_next[i, c])
 
@@ -422,18 +439,27 @@
     def mid_apply():
         us = [X1[a] for a in range(MID_NODES)]
         vs = [u + CO[0] * jnp.sum(u, axis=0, keepdims=True) for u in us]
-        yas = centro(p4["hat"], vs)
-        out = []
-        for a in range(MID_NODES):
-            yk = sublanes(vs[a], p4["along"], tab)
-            base = CO[5] * us[a] + CO[6] * yas[a] + CO[8] * yk
-            yb = centro(p4["hat"], [vs[a][:, b] for b in range(MID_NODES)])
-            rows = [
-                (base[:, b] + CO[7] * yb[b]) * float(w4[a] * w4[b]) for b in range(MID_NODES)
-            ]
-            rows[0] = rows[0] + lane_up(rows[last4])
-            out.append(jnp.stack(rows[:last4], axis=1))
-        return out
+        half = MID_NODES // 2
+        es = [vs[j] + vs[last4 - j] for j in range(half)]
+        os = [vs[j] - vs[last4 - j] for j in range(half)]
+
+        def pair(a):
+            even, odd = split(p4["hat"], a)
+            p, q = weigh(even, es), weigh(odd, os)
+            out = []
+            for plane, ya in ((a, p + q), (last4 - a, p - q)):
+                yk = sublanes(vs[plane], p4["along"], tab)
+                base = CO[5] * us[plane] + CO[6] * ya + CO[8] * yk
+                yb = centro(p4["hat"], [vs[plane][:, b] for b in range(MID_NODES)])
+                rows = [
+                    (base[:, b] + CO[7] * yb[b]) * float(w4[plane] * w4[b])
+                    for b in range(MID_NODES)
+                ]
+                rows[0] = rows[0] + lane_up(rows[last4])
+                out.append(jnp.stack(rows[:last4], axis=1))
+            return out
+
+        return pair
 
     def mid_store(a, x):
         X1[a, :, 0:last4] = x
@@ -456,8 +482,10 @@
         return arrive
 
     def mid_sweep():
-        z = mid_apply()
-        arrive = mid_exchange(z[0], z[last4])
+        pair = mid_apply()
+        faces = pair(0)
+        arrive = mid_exchange(faces[0], faces[1])
+        z = [faces[0], *pair(1), faces[1]]
 
         def update(a, total):
             mid_store(a, X1[a, :, 0:last4] + ID1[a] * (B1[a] - total))
@@ -508,11 +536,10 @@
 
         def derived(i):
             u = D[now, h + 1, i]
-            total = sublanes(u, PLAN["csum"], tab)
-            four = [
-                u, u - sublanes(u, PLAN["kswap"], tab),
-                total, total - sublanes(total, PLAN["kswap"], tab),
-            ]
+            rolled = [u] + [pltpu.roll(u, r, 0) for r in range(1, SUB)]
+            four = [u]
+            for terms in PLAN["derived"]:
+                four.append(tree([rolled[r] * tab[column] for r, column in terms]))
             return four, [lane_down(x) for x in four]
 
         carry = None
@@ -544,10 +571,11 @@
             carry = sums[1]
             left = right
 
+    fine_prepare(inner)
     fine_sweep(0, mid_setup)
 
     jf, jc = PLAN["jf"], PLAN["jc"]
-    fine_prepare()
+    fine_prepare([0])
 
     @pl.loop(0, 3)
     def _(c):
@@ -576,7 +604,9 @@
         mid_store(a, ID1[a] * b1)
 
     mid_sweep()
-    z = mid_apply()
+    pair = mid_apply()
+    faces = pair(0)
+    z = [faces[0], *pair(1), faces[1]]
     rs = [B1[a] - z[a] for a in range(last4)] + [-z[last4]]
     hs = []
     for ac in range(2):
@@ -590,11 +620,29 @@
         hs.append(total)
     HB[REACH, 0], HB[REACH, 1] = hs[0], hs[1]
     halo = [to_member(HB.at[REACH], HB.at[REACH - o], near(o)) for o in reach]
-    for copy in halo:
+    inside = REACH // 2
+    for copy in halo[: 2 * inside]:
         copy.wait_recv()
-    for i in range(PLANES):
+    mid_low, mid_high = inside, PLANES - inside
+    others = []
+
+    def planes_out(low, high):
+        for o in range(1, loops):
+            cut = min(o, loops - o)
+            first, last = max(low, cut), min(high, PLANES - cut)
+            if first < last:
+                part = pl.ds(first, last - first)
+                others.append(to_group(BP.at[part], R.at[g, part], o))
+
+    for i in range(mid_low, mid_high):
         BP[i] = HB[i + 1, 0] + HB[i, 1]
-    others = [to_group(BP, R.at[g], o) for o in range(1, loops)]
+    planes_out(mid_low, mid_high)
+    for copy in halo[2 * inside :]:
+        copy.wait_recv()
+    for i in [*range(mid_low), *range(mid_high, PLANES)]:
+        BP[i] = HB[i + 1, 0] + HB[i, 1]
+    planes_out(0, mid_low)
+    planes_out(mid_high, PLANES)
     R[g] = BP[...]
     center = 0.5 * (UPPER_BOUND + LOWER_BOUND)
     radius = 0.5 * (UPPER_BOUND - LOWER_BOUND)
@@ -613,8 +661,7 @@
         damping_next = 1.0 / (2.0 * ratio - damping_now)
         first, second = damping_next * damping_now, 2.0 * damping_next / radius
         if s < CHEB - 2:
-            @pl.loop(0, loops)
-            def _(h):
+            for h in range(loops):
                 coarse_step(s, h, first, second)
         else:
             coarse_step(s, g, first, second)
@@ -650,17 +697,12 @@
             X[c, a, 0:last8] = x
             X[c, a, last8] = lane_down(x[0])
 
+    fine_prepare(inner)
     fine_sweep(1)
     fine_sweep(2)
 
-    fine_prepare()
-
-    @pl.loop(0, 3)
-    def _(c):
-        z = fine_pair(c, 0)
-        f_dn[3, c], f_up[3, c] = z[0], z[1]
-
-    final = to_member(f_up.at[3], f_from_prev.at[3], nxt)
+    fine_prepare([0])
+    final = fine_faces(3, both=False)
 
     @pl.loop(0, 3)
     def _(c):
@@ -671,10 +713,8 @@
         for a in range(last8):
             sol[c, a] = X[c, a, 0:last8]
 
-    final.wait_recv()
-
-    @pl.loop(0, 3)
-    def _(c):
+    for c in range(3):
+        final[c][0].wait_recv()
         res[c, 0] = B0[c, 0] - FM[0] * (f_dn[3, c] + f_from_prev[3, c])
 
     for copy in pending:
@@ -690,12 +730,13 @@
         return pltpu.VMEM(shape, f32)
 
     spec = pl.BlockSpec(memory_space=pltpu.VMEM)
-    slots = 60
+    slots = 80
     loops = lax.axis_size("group")
     hbm = pl.BlockSpec(memory_space=pltpu.HBM)
     scratch = [
         vmem(3, o, o, *tile), pltpu.VMEM((o, o, 2, LANES), jnp.int32), vmem(*TABLE.shape),
-        pltpu.SemaphoreType.DMA((3,)),
+        vmem(3, LANES), vmem(1, LANES), vmem(1, LANES), vmem(1, LANES),
+        pltpu.SemaphoreType.DMA((7,)),
         vmem(3, n, n, *tile), vmem(3, n, n, *tile), vmem(3, n, n, *tile),
         vmem(3, n, o, *tile), vmem(n, o, *tile), vmem(n, o, *tile),
         vmem(n, q, *tile), vmem(q, 3, q - 1, *tile),
@@ -717,20 +758,25 @@
     return pl.pallas_call(
         kernel,
         out_shape=(shape, shape),
-        in_specs=[hbm, spec, spec, spec, hbm, spec, hbm],
+        in_specs=[hbm] * 7,
         out_specs=(spec, spec),
         scratch_shapes=scratch,
         compiler_params=pltpu.CompilerParams(
             collective_id=0, has_side_effects=True, vmem_limit_bytes=48 * 2**20
         ),
     )(
-        load,
-        stiffness_dir,
-        bulk_ratio.reshape(1, LANES),
-        thermal_shift.reshape(1, LANES),
-        contact.transpose(1, 2, 0, 3),
-        loop_tie.reshape(1, LANES),
-        jnp.asarray(TABLE),
+        *(
+            pltpu.with_memory_space_constraint(x, pltpu.HBM)
+            for x in (
+                load,
+                stiffness_dir,
+                bulk_ratio.reshape(1, LANES),
+                thermal_shift.reshape(1, LANES),
+                contact.transpose(1, 2, 0, 3),
+                loop_tie.reshape(1, LANES),
+                jnp.asarray(TABLE),
+            )
+        )
     )
 
 

time: 72.9 us -> 67.8 us (0.930)
  local copies, waits for them, and re-layouts: 5.11 us -> 1.64 us
  Pallas kernels: 66.9 us -> 65.4 us
    unnamed x16 -> x2, local copies, waits for them, and re-layouts: 5.11 us -> 1.64 us
    pallas_call x1, Pallas kernels: 66.9 us -> 65.4 us  [body(): pl.pallas_call(kernel, out_shape=(shape, shape), in_specs=[hbm] * 7, out_...]
where the time goes in v2:
time: 67.8 us; the launch traced here: 67.7 us
  Pallas kernels  65.4 us (96%)
  local copies, waits for them, and re-layouts  1.64 us (2%)
    pallas_call x1, Pallas kernels, body(): pl.pallas_call(kernel, out_shape=(shape, shape), in_specs=[hbm] * 7, out_...  65.4 us
    unnamed x2, local copies, waits for them, and re-layouts  1.64 us

profile of v2, /device:TPU:2, one launch (start us, length us, event | category | flops | bytes accessed | tf_op | source)
XLA Modules:
  0.0 67.7 jit_solution(10396773005633954797)
XLA Ops:
  0.6 65.4 %shard_map.86 = (f32[3,7,7,8,128]{4,3,2,1,0:T(8,128)S(1)}, f32[3,7,7,8,128]{4,3,2,1,0:T(8,128)S(1)}) custom-call(f32[3,7,7,8,128]{4,3,2,1,0:T(8,128)} %load_hbm.1, f32[3,128]{1,0:T(4,128)} %stiff_hbm.1, f32[1,128]{1,0:T(1,128)} %bitcast.5, f32[1,128]{1,0:T(1,128)} %bitcast.6, s32[7,7,2,128]{3,2,1,0:T(2,128)} %bitcast.4, f32[1,128]{1,0:T(1,128)} %bitcast.7, ...), custom_call_target="tpu_custom_call" | custom-call | tf_op jit(solution)/shard_map/pallas_call | solution.py:758
  66.0 0.8 %copy.11 = f32[3,7,7,8,128]{4,3,2,1,0:T(8,128)} copy(f32[3,7,7,8,128]{4,3,2,1,0:T(8,128)S(1)} %get-tuple-element.4) | data formatting | bytes 1204224
  66.9 0.8 %copy.12 = f32[3,7,7,8,128]{4,3,2,1,0:T(8,128)} copy(f32[3,7,7,8,128]{4,3,2,1,0:T(8,128)S(1)} %get-tuple-element.5) | data formatting | bytes 1204224

commit v3 on v2

--- a/solution.py
+++ b/solution.py
@@ -620,7 +620,7 @@
         hs.append(total)
     HB[REACH, 0], HB[REACH, 1] = hs[0], hs[1]
     halo = [to_member(HB.at[REACH], HB.at[REACH - o], near(o)) for o in reach]
-    inside = REACH // 2
+    inside = REACH - 2
     for copy in halo[: 2 * inside]:
         copy.wait_recv()
     mid_low, mid_high = inside, PLANES - inside
@@ -719,6 +719,18 @@
 
     for copy in pending:
         copy.wait_send()
+
+
+def write_out(sol, res, sol_hbm, res_hbm, sem):
+    copies = [
+        pltpu.make_async_copy(src.at[c], dst.at[c], sem.at[2 * c + i])
+        for c in range(3)
+        for i, (src, dst) in enumerate(((sol, sol_hbm), (res, res_hbm)))
+    ]
+    for copy in copies:
+        copy.start()
+    for copy in copies:
+        copy.wait()
 
 
 def body(load, stiffness_dir, bulk_ratio, thermal_shift, contact, loop_tie):
@@ -755,7 +767,7 @@
         pltpu.SemaphoreType.DMA((slots,)),
     ]
     shape = jax.ShapeDtypeStruct(load.shape, f32)
-    return pl.pallas_call(
+    outputs = pl.pallas_call(
         kernel,
         out_shape=(shape, shape),
         in_specs=[hbm] * 7,
@@ -778,6 +790,14 @@
             )
         )
     )
+    return pl.pallas_call(
+        write_out,
+        out_shape=(shape, shape),
+        in_specs=[spec, spec],
+        out_specs=(hbm, hbm),
+        scratch_shapes=[pltpu.SemaphoreType.DMA((6,))],
+        compiler_params=pltpu.CompilerParams(vmem_limit_bytes=2**20),
+    )(*outputs)
 
 
 def solution(mesh):

time: 67.8 us -> 67.2 us (level)
  local copies, waits for them, and re-layouts: 1.64 us -> 0 us
  Pallas kernels: 65.4 us -> 66.5 us
    unnamed x2 -> x0, local copies, waits for them, and re-layouts: 1.64 us -> none
    pallas_call x0 -> x1, Pallas kernels: none -> 1.06 us  [body(): pl.pallas_call(write_out, out_shape=(shape, shape), in_specs=[spec, spec]...]
where the time goes in v3:
time: 67.2 us
  Pallas kernels  66.5 us (99%)
    pallas_call x1, Pallas kernels, body(): pl.pallas_call(kernel, out_shape=(shape, shape), in_specs=[hbm] * 7, out_...  65.4 us

profile of v3, /device:TPU:2, one launch (start us, length us, event | category | flops | bytes accessed | tf_op | source)
XLA Modules:
  0.0 67.2 jit_solution(7894994983732023371)
XLA Ops:
  0.6 65.4 %shard_map.86 = (f32[3,7,7,8,128]{4,3,2,1,0:T(8,128)S(1)}, f32[3,7,7,8,128]{4,3,2,1,0:T(8,128)S(1)}) custom-call(f32[3,7,7,8,128]{4,3,2,1,0:T(8,128)} %load_hbm.1, f32[3,128]{1,0:T(4,128)} %stiff_hbm.1, f32[1,128]{1,0:T(1,128)} %bitcast.5, f32[1,128]{1,0:T(1,128)} %bitcast.6, s32[7,7,2,128]{3,2,1,0:T(2,128)} %bitcast.4, f32[1,128]{1,0:T(1,128)} %bitcast.7, ...), custom_call_target="tpu_custom_call" | custom-call | tf_op jit(solution)/shard_map/pallas_call | solution.py:770
  66.1 1.1 %shard_map.87 = (f32[3,7,7,8,128]{4,3,2,1,0:T(8,128)}, f32[3,7,7,8,128]{4,3,2,1,0:T(8,128)}) custom-call(f32[3,7,7,8,128]{4,3,2,1,0:T(8,128)S(1)} %get-tuple-element.4.sol, f32[3,7,7,8,128]{4,3,2,1,0:T(8,128)S(1)} %get-tuple-element.5.res), custom_call_target="tpu_custom_call" | custom-call | tf_op jit(solution)/shard_map/pallas_call | solution.py:793
